TPU v7x, 32 devices: a whole 2x2x4 slice. The times are simulated.
32 devices in a mesh: plane: 4 (over y, core), frame: 8 (over z, x).
Axes of the slice: x: 2, y: 2, z: 4, core: 2. Of those that a mesh axis runs over, the one named last changes fastest.
Arguments:
- image: float32 [8, 8, 2, 128, 128], P('plane', 'frame'), may hold values from -6 to 6
- sens: bfloat16 [4, 8, 2, 128, 128], P(None, 'plane'), may hold values from -3 to 3
- kspace: bfloat16 [4, 8, 8, 2, 128, 128], P(None, 'plane', 'frame'), may hold values from -6 to 6
- offsets: int32 [8, 128], P('frame'), may hold values from 0 to 3
- shifts: int32 [2], replicated, may hold values from 0 to 7
- step_size: float32 [1], replicated, may hold values from 0.5 to 1.5
- threshold: float32 [1], replicated, may hold values from 100 to 1000
Outputs:
- new_image: float32 [8, 8, 2, 128, 128], P('plane', 'frame')
All inputs are finite; a program needn't handle non-finite values.
Results may differ from a plain program's by a relative error of at most 0.0003.
Values sent between devices are 32-bit elements; how exact they have to be, the bound alone decides.
A program may use at most 64 MiB of HBM per device.

v0:
```python
import functools
import math

import jax
import jax.numpy as jnp
import numpy as np
from jax import lax
from jax.experimental import pallas as pl
from jax.experimental.pallas import tpu as pltpu
from jax.sharding import PartitionSpec as P

PATCH_X = 4
PATCH_Y = 8
PATCH_Z = 8
ACCEL = 4
CENTER = 8


def from_partner(block, axis, distance):
    count = lax.axis_size(axis)
    route = []
    for low in range(count):
        high = low | 1 << distance
        if high != low and high < count:
            route += [(low, high), (high, low)]
    return lax.ppermute(block, axis, route)


def dft_tables(length):
    indices = jnp.arange(length, dtype=jnp.int32)
    phases = indices[:, None] * indices[None, :] % length
    angles = phases.astype(jnp.float32) * (2.0 * math.pi / length)
    norm_scale = 1.0 / math.sqrt(length)
    return (jnp.cos(angles) * norm_scale, jnp.sin(angles) * norm_scale)


def along_z(stacked, right_table, sign, width_z):
    product = jnp.einsum(
        "...z,zw->...w",
        stacked,
        right_table,
        precision=lax.Precision.HIGHEST,
        preferred_element_type=jnp.float32,
    )
    cos_part = product[..., :width_z]
    sin_part = product[..., width_z:]
    real_part = cos_part[..., 0, :, :] + sign * sin_part[..., 1, :, :]
    imag_part = cos_part[..., 1, :, :] - sign * sin_part[..., 0, :, :]
    return jnp.stack([real_part, imag_part], axis=-3)


def along_y(stacked, left_table):
    shape_in = stacked.shape
    merged = stacked.reshape(shape_in[:-3] + (2 * shape_in[-2], shape_in[-1]))
    result = jnp.einsum(
        "ur,...rz->...uz",
        left_table,
        merged,
        precision=lax.Precision.HIGHEST,
        preferred_element_type=jnp.float32,
    )
    return result.reshape(shape_in)


def rotate(casorati):
    frames2, voxels = (casorati.shape[-2], casorati.shape[-1])
    split_parts = casorati.reshape(casorati.shape[:-2] + (frames2 // 2, 2, voxels))
    turned = jnp.stack([-split_parts[..., 1, :], split_parts[..., 0, :]], axis=-2)
    return turned.reshape(casorati.shape)


def gram_of(casorati):
    twin = rotate(casorati)
    first = jnp.einsum(
        "kav,kbv->kab",
        casorati,
        casorati,
        precision=lax.Precision.HIGHEST,
        preferred_element_type=jnp.float32,
    )
    second = jnp.einsum(
        "kav,kbv->kab",
        twin,
        twin,
        precision=lax.Precision.HIGHEST,
        preferred_element_type=jnp.float32,
    )
    return first + second


def shrink(casorati, gram, level):
    order = gram.shape[-1]
    system = gram + level * jnp.eye(order, dtype=jnp.float32)
    factor = jnp.linalg.cholesky(system)
    forward_part = jax.scipy.linalg.solve_triangular(factor, casorati, lower=True)
    solved = jax.scipy.linalg.solve_triangular(factor, forward_part, lower=True, trans=1)
    return casorati - level * solved


def local_general(image, sens, kspace, offsets, shifts, step_size, threshold):
    planes, frames_dev, _, width_y, width_z = image.shape
    frames = frames_dev * lax.axis_size("frame")
    cos_y, sin_y = dft_tables(width_y)
    cos_z, sin_z = dft_tables(width_z)
    right_table = jnp.concatenate([cos_z, sin_z], axis=1)
    left_forward = jnp.concatenate(
        [jnp.concatenate([cos_y, sin_y], axis=1), jnp.concatenate([-sin_y, cos_y], axis=1)], axis=0
    )
    left_inverse = jnp.concatenate(
        [jnp.concatenate([cos_y, -sin_y], axis=1), jnp.concatenate([sin_y, cos_y], axis=1)], axis=0
    )
    rows_y = jnp.arange(width_y, dtype=jnp.int32)
    rows_z = jnp.arange(width_z, dtype=jnp.int32)
    low_y = (rows_y < CENTER) | (rows_y >= width_y - CENTER)
    low_z = (rows_z < CENTER) | (rows_z >= width_z - CENTER)
    regular = (rows_z[None, None, :] + offsets[:, :, None]) % ACCEL == 0
    sampled = (regular | low_y[None, :, None] & low_z[None, None, :]).astype(jnp.float32)
    image_re = image[:, :, 0]
    image_im = image[:, :, 1]
    maps = sens.astype(jnp.float32)
    sens_re = maps[:, :, 0][:, :, None]
    sens_im = maps[:, :, 1][:, :, None]
    coil_re = sens_re * image_re[None] - sens_im * image_im[None]
    coil_im = sens_re * image_im[None] + sens_im * image_re[None]
    stacked = jnp.stack([coil_re, coil_im], axis=3)
    spectra = along_y(along_z(stacked, right_table, 1.0, width_z), left_forward)
    resid = sampled[None, None, :, None] * (spectra - kspace.astype(jnp.float32))
    returned = along_z(along_y(resid, left_inverse), right_table, -1.0, width_z)
    back_re = returned[:, :, :, 0]
    back_im = returned[:, :, :, 1]
    grad_re = jnp.sum(sens_re * back_re + sens_im * back_im, axis=0)
    grad_im = jnp.sum(sens_re * back_im - sens_im * back_re, axis=0)
    moved = image - step_size[0] * jnp.stack([grad_re, grad_im], axis=2)
    rolled = jnp.roll(moved, (shifts[0], shifts[1]), axis=(3, 4))
    nyb = width_y // PATCH_Y
    nzb = width_z // PATCH_Z
    voxels = planes * PATCH_Y * PATCH_Z
    blocks = rolled.reshape(planes, frames_dev, 2, nyb, PATCH_Y, nzb, PATCH_Z)
    blocks = blocks.transpose(3, 5, 1, 2, 0, 4, 6).reshape(nyb * nzb, frames_dev, 2, voxels)
    regrouped = lax.all_to_all(blocks, "frame", split_axis=0, concat_axis=1, tiled=True)
    count = regrouped.shape[0]
    casorati = regrouped.reshape(count, 2 * frames, voxels)
    level = threshold[0]
    parity = lax.axis_index("plane") % 2
    halfway = count // 2
    first_part = casorati[:halfway]
    second_part = casorati[halfway:]
    kept_part = jnp.where(parity == 0, first_part, second_part)
    outgoing = jnp.where(parity == 0, second_part, first_part)
    incoming = from_partner(outgoing, "plane", 0)
    complete = jnp.concatenate([kept_part, incoming], axis=2)
    finished = shrink(complete, gram_of(complete), level)
    own_part = finished[:, :, :voxels]
    returned_part = from_partner(finished[:, :, voxels:], "plane", 0)
    shrunk = jnp.where(
        parity == 0,
        jnp.concatenate([own_part, returned_part], axis=0),
        jnp.concatenate([returned_part, own_part], axis=0),
    )
    restored = lax.all_to_all(
        shrunk.reshape(count, frames, 2, voxels), "frame", split_axis=1, concat_axis=0, tiled=True
    )
    placed = restored.reshape(nyb, nzb, frames_dev, 2, planes, PATCH_Y, PATCH_Z)
    placed = placed.transpose(4, 2, 3, 0, 5, 1, 6).reshape(planes, frames_dev, 2, width_y, width_z)
    return jnp.roll(placed, (-shifts[0], -shifts[1]), axis=(3, 4))


VMEM_BYTES = 24 * 1024 * 1024


def block_tables(length):
    indices = np.arange(length)
    angles = (indices[:, None] * indices[None, :] % length) * (2.0 * np.pi / length)
    cos = np.cos(angles) / np.sqrt(length)
    sin = np.sin(angles) / np.sqrt(length)
    parts = []
    for table in (cos, sin):
        high = table.astype(jnp.bfloat16)
        parts += [high, (table - high.astype(np.float64)).astype(jnp.bfloat16)]
    return np.stack(parts)


def lay_tables(parts_ref, table_ref, width):
    low, top = pl.ds(0, width), pl.ds(width, width)
    for k in range(2):
        cos, sin = parts_ref[k], parts_ref[2 + k]
        for table, upper, lower in ((k, sin, -sin), (2 + k, -sin, sin)):
            table_ref[table, low, low] = cos
            table_ref[table, top, top] = cos
            table_ref[table, low, top] = upper
            table_ref[table, top, low] = lower


def halves(values):
    high = values.astype(jnp.bfloat16)
    return high, (values - high.astype(jnp.float32)).astype(jnp.bfloat16)


def mul(left, right):
    return jnp.dot(left, right, preferred_element_type=jnp.float32)


def from_right(values, high, low):
    value_high, value_low = halves(values)
    return mul(value_high, high) + mul(value_high, low) + mul(value_low, high)


def from_left(high, low, values):
    value_high, value_low = halves(values)
    return mul(high, value_high) + mul(low, value_high) + mul(high, value_low)


def rows_to_lanes(values, coils, width):
    parts = [
        jnp.concatenate([values[c * width : (c + 1) * width, k * width : (k + 1) * width] for c in range(coils)], axis=1)
        for k in range(2)
    ]
    return jnp.concatenate(parts, axis=0)


def lanes_to_rows(values, coils, width):
    parts = [
        jnp.concatenate([values[k * width : (k + 1) * width, c * width : (c + 1) * width] for k in range(2)], axis=1)
        for c in range(coils)
    ]
    return jnp.concatenate(parts, axis=0)


def moved_plane(loads, start_later, p, coils, width, image_ref, sens_ref, kspace_ref, table_ref, step, sampled):
    loads["image", p].wait()
    loads["sens", p].wait()
    image_re = image_ref[p, 0, 0]
    image_im = image_ref[p, 0, 1]
    stacked = []
    for c in range(coils):
        sens_re = sens_ref[c, p, 0].astype(jnp.float32)
        sens_im = sens_ref[c, p, 1].astype(jnp.float32)
        stacked.append(
            jnp.concatenate(
                [sens_re * image_re - sens_im * image_im, sens_re * image_im + sens_im * image_re], axis=1
            )
        )
    along = from_right(jnp.concatenate(stacked, axis=0), table_ref[2], table_ref[3])
    spectra = from_left(table_ref[0], table_ref[1], rows_to_lanes(along, coils, width))
    loads["kspace", p].wait()
    if p == 0:
        start_later()
    data = jnp.concatenate(
        [
            jnp.concatenate([kspace_ref[c, p, 0, k].astype(jnp.float32) for c in range(coils)], axis=1)
            for k in range(2)
        ],
        axis=0,
    )
    weight = jnp.concatenate([jnp.concatenate([sampled] * coils, axis=1)] * 2, axis=0)
    resid = weight * (spectra - data)
    back = from_left(table_ref[2], table_ref[3], resid)
    returned = from_right(lanes_to_rows(back, coils, width), table_ref[0], table_ref[1])
    grad_re = jnp.zeros_like(image_re)
    grad_im = jnp.zeros_like(image_im)
    for c in range(coils):
        back_re = returned[c * width : (c + 1) * width, :width]
        back_im = returned[c * width : (c + 1) * width, width:]
        sens_re = sens_ref[c, p, 0].astype(jnp.float32)
        sens_im = sens_ref[c, p, 1].astype(jnp.float32)
        grad_re += sens_re * back_re + sens_im * back_im
        grad_im += sens_re * back_im - sens_im * back_re
    return image_re - step * grad_re, image_im - step * grad_im


def sweep(matrix, order):
    for k in range(order):
        pivot = 1.0 / matrix[k, k][0]
        column = {}
        for i in range(order):
            if i > k:
                column[i] = matrix[i, k]
            elif i < k:
                column[i] = (matrix[k, i][0], -matrix[k, i][1])
        scaled = {i: (re * pivot, im * pivot) for i, (re, im) in column.items()}
        for i in column:
            for j in column:
                if j > i:
                    continue
                a_re, a_im = scaled[i]
                b_re, b_im = column[j]
                re, im = matrix[i, j]
                re = re - (a_re * b_re + a_im * b_im)
                if i != j:
                    im = im - (a_im * b_re - a_re * b_im)
                matrix[i, j] = (re, im)
        for i in column:
            if i > k:
                matrix[i, k] = scaled[i]
            else:
                matrix[k, i] = (scaled[i][0], -scaled[i][1])
        matrix[k, k] = (-pivot, None)
    return matrix


def step_kernel(
    planes, frames, group, coils, width_y, width_z,
    shifts_ref, step_ref, level_ref, offsets_ref, image_hbm, sens_hbm, kspace_hbm, table_hbm,
    landed,
    image_ref, sens_ref, kspace_ref, parts_ref, table_ref, load_sem,
    wrapped, rolled, gathered, entries, inverse, finished,
    send_out, recv_out, send_back, recv_back, own_out, own_back,
):
    total = frames * group
    plane_me = lax.axis_index("plane")
    frame_me = lax.axis_index("frame")
    part_me = lax.rem(plane_me, group)
    base = plane_me - part_me
    me = frame_me * group + part_me
    rows = PATCH_Y

    def flip(index, mask, count):
        bit = 1
        while bit < count:
            if mask & bit:
                index = index + bit - 2 * bit * lax.rem(index // bit, 2)
            bit *= 2
        return index

    def device(index):
        return {"plane": base + lax.rem(index, group), "frame": index // group}

    loads = {}

    def load(name, source, target):
        loads[name] = pltpu.make_async_copy(source, target, load_sem.at[len(loads)])
        loads[name].start()

    def load_plane(p):
        load(("image", p), image_hbm.at[p], image_ref.at[p])
        load(("sens", p), sens_hbm.at[:, p], sens_ref.at[:, p])
        load(("kspace", p), kspace_hbm.at[:, p], kspace_ref.at[:, p])

    def start_later():
        for p in range(1, planes):
            load_plane(p)

    load("table", table_hbm, parts_ref)
    load_plane(0)

    barrier = pltpu.get_barrier_semaphore()
    for k in range(1, total):
        pl.semaphore_signal(barrier, inc=1, device_id=device(flip(me, k, total)), device_id_type=pl.DeviceIdType.MESH)

    lane = lax.broadcasted_iota(jnp.int32, (width_y, width_z), 1)
    row = lax.broadcasted_iota(jnp.int32, (width_y, width_z), 0)
    offset = jnp.broadcast_to(offsets_ref[...].astype(jnp.float32), (width_z, width_y)).T
    wanted = jnp.where(offset == 0.0, 0.0, ACCEL - offset)
    regular = lax.rem(lane, ACCEL).astype(jnp.float32) == wanted
    low_y = (row < CENTER) | (row >= width_y - CENTER)
    low_z = (lane < CENTER) | (lane >= width_z - CENTER)
    sampled = (regular | (low_y & low_z)).astype(jnp.float32)

    sends = []
    loads["table"].wait()
    lay_tables(parts_ref, table_ref, width_y)
    for p in range(planes):
        moved = moved_plane(loads, start_later, p, coils, width_y, image_ref, sens_ref, kspace_ref, table_ref, step_ref[0], sampled)
        for k in range(2):
            part = pltpu.roll(moved[k], shifts_ref[1], 1)
            wrapped[p, k, pl.ds(0, rows), :] = part[width_y - rows :]
            wrapped[p, k, pl.ds(rows, width_y), :] = part
            rolled[p, k] = wrapped[p, k, pl.ds(rows - shifts_ref[0], width_y), :]
        if p == 0:
            pl.semaphore_wait(barrier, total - 1)
        group_sends = []
        for k in reversed(range(1, total)):
            target = flip(me, k, total)
            copy = pltpu.make_async_remote_copy(
                src_ref=rolled.at[p, :, pl.ds(pl.multiple_of(target * rows, rows), rows), :],
                dst_ref=gathered.at[p, part_me, frame_me],
                send_sem=send_out.at[p, k],
                recv_sem=recv_out.at[p, k],
                device_id=device(target),
                device_id_type=pl.DeviceIdType.MESH,
            )
            copy.start()
            group_sends.append(copy)
        own = pltpu.make_async_copy(
            rolled.at[p, :, pl.ds(pl.multiple_of(me * rows, rows), rows), :],
            gathered.at[p, part_me, frame_me],
            own_out.at[p],
        )
        own.start()
        sends.append((group_sends, own))

    pairs = [(f, g) for f in range(frames) for g in range(f + 1)]
    for p in range(planes):
        group_sends, own = sends[p]
        own.wait()
        for copy in group_sends:
            copy.wait_recv()
        for n, (f, g) in enumerate(pairs):
            sum_re = None
            sum_im = None
            for q in range(group):
                f_re, f_im = gathered[p, q, f, 0], gathered[p, q, f, 1]
                g_re, g_im = gathered[p, q, g, 0], gathered[p, q, g, 1]
                re = f_re * g_re + f_im * g_im
                sum_re = re if sum_re is None else sum_re + re
                if f != g:
                    im = f_im * g_re - f_re * g_im
                    sum_im = im if sum_im is None else sum_im + im
            spot = f * frames + g
            entries[spot] = sum_re if p == 0 else entries[spot] + sum_re
            if f != g:
                spot = g * frames + f
                entries[spot] = sum_im if p == 0 else entries[spot] + sum_im

    one_row = lax.broadcasted_iota(jnp.int32, (width_z, width_z), 0) // PATCH_Z
    one_lane = lax.broadcasted_iota(jnp.int32, (width_z, width_z), 1) // PATCH_Z
    same = (one_row == one_lane).astype(jnp.bfloat16)
    cells = entries[...]
    shift = rows // 2
    while shift:
        cells = cells + pltpu.roll(cells, shift, 1)
        shift //= 2
    high, low = halves(cells.reshape(frames * frames * rows, width_z))
    entries[...] = (mul(high, same) + mul(low, same)).reshape(frames * frames, rows, width_z)

    level = level_ref[0]
    matrix = {}
    for f, g in pairs:
        if f == g:
            matrix[f, f] = (entries[f * frames + f] + level, None)
        else:
            matrix[f, g] = (entries[f * frames + g], entries[g * frames + f])
    matrix = sweep(matrix, frames)
    for f, g in pairs:
        re, im = matrix[f, g]
        inverse[f, g, 0] = re * level
        if f != g:
            inverse[f, g, 1] = im * level
            inverse[g, f, 0] = re * level
            inverse[g, f, 1] = -im * level
        else:
            inverse[f, f, 1] = jnp.zeros_like(re)

    backs = []
    spot = pl.ds(pl.multiple_of(me * rows, rows), rows)
    for k in reversed(range(frames)):
        f = flip(frame_me, k, frames)
        weights = [(inverse[f, g, 0], inverse[f, g, 1]) for g in range(frames)]
        for r in reversed(range(group)):
            q = flip(part_me, r, group)
            for p in range(planes):
                re = gathered[p, q, f, 0]
                im = gathered[p, q, f, 1]
                for g in range(frames):
                    g_re, g_im = gathered[p, q, g, 0], gathered[p, q, g, 1]
                    w_re, w_im = weights[g]
                    re = re + (w_re * g_re - w_im * g_im)
                    im = im + (w_re * g_im + w_im * g_re)
                finished[q, f, p, 0] = re
                finished[q, f, p, 1] = im
            if k == 0 and r == 0:
                copy = pltpu.make_async_copy(finished.at[q, f], landed.at[:, 0, :, spot, :], own_back)
            else:
                copy = pltpu.make_async_remote_copy(
                    src_ref=finished.at[q, f],
                    dst_ref=landed.at[:, 0, :, spot, :],
                    send_sem=send_back.at[r, k],
                    recv_sem=recv_back.at[r, k],
                    device_id={"plane": base + q, "frame": f},
                    device_id_type=pl.DeviceIdType.MESH,
                )
            copy.start()
            backs.append((copy, k == 0 and r == 0))
    for copy, local in backs:
        if local:
            copy.wait()
        else:
            copy.wait_recv()
    for group_sends, own in sends:
        for copy in group_sends:
            copy.wait_send()
    for copy, local in backs:
        if not local:
            copy.wait_send()


def unroll_kernel(planes, width_y, width_z, shifts_ref, landed_ref, out_ref, wrapped):
    shift_z = lax.rem(width_z - shifts_ref[1], width_z)
    for p in range(planes):
        for k in range(2):
            part = pltpu.roll(landed_ref[p, 0, k], shift_z, 1)
            wrapped[p, k, pl.ds(0, width_y), :] = part
            wrapped[p, k, pl.ds(width_y, PATCH_Y), :] = part[:PATCH_Y]
            out_ref[p, 0, k] = wrapped[p, k, pl.ds(shifts_ref[0], width_y), :]


def local_fused(image, sens, kspace, offsets, shifts, step_size, threshold):
    planes, _, _, width_y, width_z = image.shape
    coils = sens.shape[0]
    frames = lax.axis_size("frame")
    group = PATCH_X // planes
    total = frames * group
    table = jnp.asarray(block_tables(width_y))
    vmem = pl.BlockSpec(memory_space=pltpu.VMEM)
    smem = pl.BlockSpec(memory_space=pltpu.SMEM)
    hbm = pl.BlockSpec(memory_space=pltpu.HBM)
    slab = (PATCH_Y, width_z)
    dma = pltpu.SemaphoreType.DMA
    image, sens, kspace, table = [pltpu.with_memory_space_constraint(x, pltpu.HBM) for x in (image, sens, kspace, table)]
    landed = pl.pallas_call(
        functools.partial(step_kernel, planes, frames, group, coils, width_y, width_z),
        out_shape=jax.ShapeDtypeStruct(image.shape, jnp.float32),
        in_specs=[smem, smem, smem, vmem, hbm, hbm, hbm, hbm],
        out_specs=pl.BlockSpec(memory_space=pl.ANY),
        scratch_shapes=[
            pltpu.VMEM(image.shape, image.dtype),
            pltpu.VMEM(sens.shape, sens.dtype),
            pltpu.VMEM(kspace.shape, kspace.dtype),
            pltpu.VMEM(table.shape, table.dtype),
            pltpu.VMEM((4, 2 * width_y, 2 * width_y), table.dtype),
            dma((3 * planes + 1,)),
            pltpu.VMEM((planes, 2, width_y + PATCH_Y, width_z), jnp.float32),
            pltpu.VMEM((planes, 2, width_y, width_z), jnp.float32),
            pltpu.VMEM((planes, group, frames, 2) + slab, jnp.float32),
            pltpu.VMEM((frames * frames,) + slab, jnp.float32),
            pltpu.VMEM((frames, frames, 2) + slab, jnp.float32),
            pltpu.VMEM((group, frames, planes, 2) + slab, jnp.float32),
            dma((planes, total)),
            dma((planes, total)),
            dma((group, frames)),
            dma((group, frames)),
            dma((planes,)),
            dma(()),
        ],
        compiler_params=pltpu.CompilerParams(collective_id=0, has_side_effects=True, vmem_limit_bytes=VMEM_BYTES),
        name="prox_step",
    )(shifts, step_size, threshold, offsets, image, sens, kspace, table)
    return pl.pallas_call(
        functools.partial(unroll_kernel, planes, width_y, width_z),
        out_shape=jax.ShapeDtypeStruct(image.shape, jnp.float32),
        in_specs=[smem, vmem],
        out_specs=vmem,
        scratch_shapes=[pltpu.VMEM((planes, 2, width_y + PATCH_Y, width_z), jnp.float32)],
        compiler_params=pltpu.CompilerParams(vmem_limit_bytes=VMEM_BYTES),
        name="shift_back",
    )(shifts, landed)


def local(image, sens, kspace, offsets, shifts, step_size, threshold):
    planes, frames_dev, _, width_y, width_z = image.shape
    frames = frames_dev * lax.axis_size("frame")
    group = PATCH_X // planes
    one_block = frames * group * PATCH_Y == width_y and frames_dev == 1 and frames & (frames - 1) == 0
    split = group > 1 and group & (group - 1) == 0 and lax.axis_size("plane") % group == 0
    if one_block and split and width_y == width_z and width_z % 128 == 0:
        return local_fused(image, sens, kspace, offsets, shifts, step_size, threshold)
    return local_general(image, sens, kspace, offsets, shifts, step_size, threshold)


def solution(mesh):
    in_specs = (
        P("plane", "frame", None, None, None),
        P(None, "plane", None, None, None),
        P(None, "plane", "frame", None, None, None),
        P("frame", None),
        P(),
        P(),
        P(),
    )
    out_specs = P("plane", "frame", None, None, None)
    return jax.shard_map(local, mesh=mesh, in_specs=in_specs, out_specs=out_specs, check_vma=False)
```

profile of v0, /device:TPU:0, one launch (start us, length us, event | category | flops | bytes accessed | tf_op | source)
XLA Modules:
  0.0 25.9 jit_solution(6485170639790242673)
XLA Ops:
  0.7 0.0 copy-start
  0.7 0.0 copy-start.1
  1.3 0.0 copy-done
  1.3 0.0 copy-done.1
  1.4 23.1 %prox_step.1.landed_ref = f32[2,1,2,128,128]{4,3,2,1,0:T(8,128)S(1)} custom-call(s32[2]{0:T(128)S(1)} %copy-done, f32[1]{0:T(128)S(6)} %copy.9.step_ref, f32[1]{0:T(128)S(6)} %copy.10.level_ref, s32[1,128]{1,0:T(1,128)S(1)} %copy-done.1, f32[2,1,2,128,128]{4,3,2,1,0:T(8,128)} %image_hbm.1, bf16[4,2,2,128,128]{4,3,2,1,0:T(8,128)(2,1)} %sens_hbm.1, ...), custom_call_target="tpu_custom_call" | custom-call | tf_op jit(solution)/shard_map/prox_step/pallas_call | solution.py:510
  24.5 1.4 %shift_back.1 = f32[2,1,2,128,128]{4,3,2,1,0:T(8,128)} custom-call(s32[2]{0:T(128)S(1)} %copy-done, f32[2,1,2,128,128]{4,3,2,1,0:T(8,128)S(1)} %prox_step.1.landed_ref), custom_call_target="tpu_custom_call" | custom-call | tf_op jit(solution)/shard_map/shift_back/pallas_call | solution.py:538
Async XLA Ops:
  0.7 0.7 %copy-start = (s32[2]{0:T(128)S(1)}, s32[2]{0:T(128)}, u32[]{:S(2)}) copy-start(s32[2]{0:T(128)} %shifts_ref.3) | copy-start | bytes 28
  0.7 0.7 %copy-start.1 = (s32[1,128]{1,0:T(1,128)S(1)}, s32[1,128]{1,0:T(1,128)}, u32[]{:S(2)}) copy-start(s32[1,128]{1,0:T(1,128)} %offsets_ref.1) | copy-start | bytes 1540
where the time goes:
time: 26 us; the launch traced here: 25.9 us
  Pallas kernels  24.5 us (94%)
  between operations  1.36 us (5%)
    pallas_call x1, Pallas kernels, local_fused(): pl.pallas_call(functools.partial(step_kernel, planes, frames, group, coil...  23.1 us
    pallas_call x1, Pallas kernels, local_fused(): pl.pallas_call(functools.partial(unroll_kernel, planes, width_y, width_z)...  1.39 us

commit v1 on v0

--- a/solution.py
+++ b/solution.py
@@ -443,11 +443,9 @@
 
     backs = []
     spot = pl.ds(pl.multiple_of(me * rows, rows), rows)
-    for k in reversed(range(frames)):
-        f = flip(frame_me, k, frames)
+    for f in range(frames):
         weights = [(inverse[f, g, 0], inverse[f, g, 1]) for g in range(frames)]
-        for r in reversed(range(group)):
-            q = flip(part_me, r, group)
+        for q in range(group):
             for p in range(planes):
                 re = gathered[p, q, f, 0]
                 im = gathered[p, q, f, 1]
@@ -458,29 +456,34 @@
                     im = im + (w_re * g_im + w_im * g_re)
                 finished[q, f, p, 0] = re
                 finished[q, f, p, 1] = im
-            if k == 0 and r == 0:
-                copy = pltpu.make_async_copy(finished.at[q, f], landed.at[:, 0, :, spot, :], own_back)
-            else:
-                copy = pltpu.make_async_remote_copy(
-                    src_ref=finished.at[q, f],
-                    dst_ref=landed.at[:, 0, :, spot, :],
-                    send_sem=send_back.at[r, k],
-                    recv_sem=recv_back.at[r, k],
-                    device_id={"plane": base + q, "frame": f},
-                    device_id_type=pl.DeviceIdType.MESH,
-                )
-            copy.start()
-            backs.append((copy, k == 0 and r == 0))
-    for copy, local in backs:
-        if local:
-            copy.wait()
-        else:
-            copy.wait_recv()
+            mine = (frame_me == f) & (part_me == q)
+            local = pltpu.make_async_copy(finished.at[q, f], landed.at[:, 0, :, spot, :], own_back)
+            copy = pltpu.make_async_remote_copy(
+                src_ref=finished.at[q, f],
+                dst_ref=landed.at[:, 0, :, spot, :],
+                send_sem=send_back.at[q, f],
+                recv_sem=recv_back.at[part_me, frame_me],
+                device_id={"plane": base + q, "frame": f},
+                device_id_type=pl.DeviceIdType.MESH,
+            )
+            pl.when(mine)(local.start)
+            pl.when(jnp.logical_not(mine))(copy.start)
+            backs.append((mine, copy))
+    local.wait()
+    for f in range(frames):
+        for q in range(group):
+            other = jnp.logical_not((frame_me == f) & (part_me == q))
+            copy = pltpu.make_async_remote_copy(
+                src_ref=finished.at[q, f],
+                dst_ref=landed.at[:, 0, :, pl.ds((f * group + q) * rows, rows), :],
+                send_sem=send_back.at[q, f],
+                recv_sem=recv_back.at[q, f],
+                device_id={"plane": base + q, "frame": f},
+                device_id_type=pl.DeviceIdType.MESH,
+            )
+            pl.when(other)(copy.wait)
     for group_sends, own in sends:
         for copy in group_sends:
-            copy.wait_send()
-    for copy, local in backs:
-        if not local:
             copy.wait_send()
 
 

time: 26 us -> 23.8 us (0.915)
  Pallas kernels: 24.5 us -> 22.3 us
    pallas_call x1, Pallas kernels: 23.1 us -> 20.9 us  [local_fused(): pl.pallas_call(functools.partial(step_kernel, planes, frames, group, coil...]
where the time goes in v1:
time: 23.8 us; the launch traced here: 23.7 us
  Pallas kernels  22.3 us (94%)
  between operations  1.36 us (6%)
    pallas_call x1, Pallas kernels, local_fused(): pl.pallas_call(functools.partial(step_kernel, planes, frames, group, coil...  20.9 us
    pallas_call x1, Pallas kernels, local_fused(): pl.pallas_call(functools.partial(unroll_kernel, planes, width_y, width_z)...  1.39 us

profile of v1, /device:TPU:0, one launch (start us, length us, event | category | flops | bytes accessed | tf_op | source)
XLA Modules:
  0.0 23.7 jit_solution(8743293611697273159)
XLA Ops:
  0.7 0.0 copy-start
  0.7 0.0 copy-start.1
  1.3 0.0 copy-done
  1.3 0.0 copy-done.1
  1.4 20.9 %prox_step.1.landed_ref = f32[2,1,2,128,128]{4,3,2,1,0:T(8,128)S(1)} custom-call(s32[2]{0:T(128)S(1)} %copy-done, f32[1]{0:T(128)S(6)} %copy.9.step_ref, f32[1]{0:T(128)S(6)} %copy.10.level_ref, s32[1,128]{1,0:T(1,128)S(1)} %copy-done.1, f32[2,1,2,128,128]{4,3,2,1,0:T(8,128)} %image_hbm.1, bf16[4,2,2,128,128]{4,3,2,1,0:T(8,128)(2,1)} %sens_hbm.1, ...), custom_call_target="tpu_custom_call" | custom-call | tf_op jit(solution)/shard_map/prox_step/pallas_call | solution.py:513
  22.3 1.4 %shift_back.1 = f32[2,1,2,128,128]{4,3,2,1,0:T(8,128)} custom-call(s32[2]{0:T(128)S(1)} %copy-done, f32[2,1,2,128,128]{4,3,2,1,0:T(8,128)S(1)} %prox_step.1.landed_ref), custom_call_target="tpu_custom_call" | custom-call | tf_op jit(solution)/shard_map/shift_back/pallas_call | solution.py:541
Async XLA Ops:
  0.7 0.7 %copy-start = (s32[2]{0:T(128)S(1)}, s32[2]{0:T(128)}, u32[]{:S(2)}) copy-start(s32[2]{0:T(128)} %shifts_ref.3) | copy-start | bytes 28
  0.7 0.7 %copy-start.1 = (s32[1,128]{1,0:T(1,128)S(1)}, s32[1,128]{1,0:T(1,128)}, u32[]{:S(2)}) copy-start(s32[1,128]{1,0:T(1,128)} %offsets_ref.1) | copy-start | bytes 1540

commit v2 on v1

--- a/solution.py
+++ b/solution.py
@@ -168,6 +168,9 @@
 VMEM_BYTES = 24 * 1024 * 1024
 
 
+ORDERS = ('near', 'near')
+
+
 def block_tables(length):
     indices = np.arange(length)
     angles = (indices[:, None] * indices[None, :] % length) * (2.0 * np.pi / length)
@@ -210,62 +213,100 @@
     return mul(high, value_high) + mul(low, value_high) + mul(high, value_low)
 
 
-def rows_to_lanes(values, coils, width):
-    parts = [
-        jnp.concatenate([values[c * width : (c + 1) * width, k * width : (k + 1) * width] for c in range(coils)], axis=1)
-        for k in range(2)
-    ]
-    return jnp.concatenate(parts, axis=0)
-
-
-def lanes_to_rows(values, coils, width):
-    parts = [
-        jnp.concatenate([values[k * width : (k + 1) * width, c * width : (c + 1) * width] for k in range(2)], axis=1)
-        for c in range(coils)
-    ]
-    return jnp.concatenate(parts, axis=0)
-
-
-def moved_plane(loads, start_later, p, coils, width, image_ref, sens_ref, kspace_ref, table_ref, step, sampled):
+def row_patterns(offsets_ref, offset_rows, width_y, width_z):
+    lane = lax.broadcasted_iota(jnp.int32, (width_y, width_z), 1)
+    row = lax.broadcasted_iota(jnp.int32, (width_y, width_z), 0)
+    offset = jnp.broadcast_to(offsets_ref[...].astype(jnp.float32), (width_z, width_y)).T
+    wanted = jnp.where(offset == 0.0, 0.0, ACCEL - offset)
+    regular = lax.rem(lane, ACCEL).astype(jnp.float32) == wanted
+    low_y = (row < CENTER) | (row >= width_y - CENTER)
+    low_z = (lane < CENTER) | (lane >= width_z - CENTER)
+    centre = low_y & low_z
+    scale = float(ACCEL)
+    kept = jnp.where(regular | centre, scale, 0.0).astype(jnp.bfloat16)
+    extra = jnp.where(centre & jnp.logical_not(regular), scale, 0.0)
+    edge = jnp.concatenate([extra[:CENTER], extra[width_y - CENTER :]], axis=0)
+    half = jnp.where((offset == 0.0) | (offset == 2.0), 1.0, -1.0)
+    real = jnp.where(offset == 0.0, 1.0, jnp.where(offset == 2.0, -1.0, 0.0))
+    imag = jnp.where(offset == 1.0, -1.0, jnp.where(offset == 3.0, 1.0, 0.0))
+    return kept, edge, half, real, imag
+
+
+def moved_plane(loads, p, coils, width, image_ref, sens_ref, kspace_ref, table_ref, step, patterns):
+    kept, edge, half, real, imag = patterns
+    loads["kspace", p].wait()
+    data = jnp.concatenate(
+        [
+            jnp.concatenate([kspace_ref[c, p, 0, k] * kept for k in range(2)], axis=1)
+            for c in range(coils)
+        ],
+        axis=0,
+    )
+    known = mul(data, table_ref[0]) + mul(data, table_ref[1])
     loads["image", p].wait()
     loads["sens", p].wait()
     image_re = image_ref[p, 0, 0]
     image_im = image_ref[p, 0, 1]
-    stacked = []
+    coil_re, coil_im = [], []
     for c in range(coils):
         sens_re = sens_ref[c, p, 0].astype(jnp.float32)
         sens_im = sens_ref[c, p, 1].astype(jnp.float32)
-        stacked.append(
+        coil_re.append(sens_re * image_re - sens_im * image_im)
+        coil_im.append(sens_re * image_im + sens_im * image_re)
+    stacked = jnp.concatenate([jnp.concatenate(coil_re, axis=1), jnp.concatenate(coil_im, axis=1)], axis=0)
+    lines = from_left(table_ref[0], table_ref[1], stacked)
+
+    def part(k, c):
+        return lines[k * width : (k + 1) * width, c * width : (c + 1) * width]
+
+    low = jnp.concatenate(
+        [
             jnp.concatenate(
-                [sens_re * image_re - sens_im * image_im, sens_re * image_im + sens_im * image_re], axis=1
+                [jnp.concatenate([part(k, c)[:CENTER], part(k, c)[width - CENTER :]], axis=0) for k in range(2)], axis=1
             )
-        )
-    along = from_right(jnp.concatenate(stacked, axis=0), table_ref[2], table_ref[3])
-    spectra = from_left(table_ref[0], table_ref[1], rows_to_lanes(along, coils, width))
-    loads["kspace", p].wait()
-    if p == 0:
-        start_later()
-    data = jnp.concatenate(
-        [
-            jnp.concatenate([kspace_ref[c, p, 0, k].astype(jnp.float32) for c in range(coils)], axis=1)
-            for k in range(2)
+            for c in range(coils)
         ],
         axis=0,
     )
-    weight = jnp.concatenate([jnp.concatenate([sampled] * coils, axis=1)] * 2, axis=0)
-    resid = weight * (spectra - data)
+    weight = jnp.concatenate([jnp.concatenate([edge] * 2, axis=1)] * coils, axis=0)
+    added = from_right(weight * from_right(low, table_ref[2], table_ref[3]), table_ref[0], table_ref[1])
+    resid_re, resid_im = [], []
+    for c in range(coils):
+        both = []
+        for k in range(2):
+            line = part(k, c)
+            both.append(line + half * pltpu.roll(line, width // 2, 1))
+        turned = [pltpu.roll(line, width // 4, 1) for line in both]
+        sums = [
+            both[0] + (real * turned[0] - imag * turned[1]),
+            both[1] + (real * turned[1] + imag * turned[0]),
+        ]
+        for k, out in ((0, resid_re), (1, resid_im)):
+            value = sums[k] - known[c * width : (c + 1) * width, k * width : (k + 1) * width]
+            more = added[2 * CENTER * c : 2 * CENTER * (c + 1), k * width : (k + 1) * width]
+            out.append(
+                jnp.concatenate(
+                    [
+                        value[:CENTER] + more[:CENTER],
+                        value[CENTER : width - CENTER],
+                        value[width - CENTER :] + more[CENTER:],
+                    ],
+                    axis=0,
+                )
+            )
+    resid = jnp.concatenate([jnp.concatenate(resid_re, axis=1), jnp.concatenate(resid_im, axis=1)], axis=0)
     back = from_left(table_ref[2], table_ref[3], resid)
-    returned = from_right(lanes_to_rows(back, coils, width), table_ref[0], table_ref[1])
     grad_re = jnp.zeros_like(image_re)
     grad_im = jnp.zeros_like(image_im)
     for c in range(coils):
-        back_re = returned[c * width : (c + 1) * width, :width]
-        back_im = returned[c * width : (c + 1) * width, width:]
+        back_re = back[:width, c * width : (c + 1) * width]
+        back_im = back[width:, c * width : (c + 1) * width]
         sens_re = sens_ref[c, p, 0].astype(jnp.float32)
         sens_im = sens_ref[c, p, 1].astype(jnp.float32)
         grad_re += sens_re * back_re + sens_im * back_im
         grad_im += sens_re * back_im - sens_im * back_re
-    return image_re - step * grad_re, image_im - step * grad_im
+    scaled = step * (1.0 / ACCEL)
+    return image_re - scaled * grad_re, image_im - scaled * grad_im
 
 
 def sweep(matrix, order):
@@ -300,11 +341,11 @@
 
 def step_kernel(
     planes, frames, group, coils, width_y, width_z,
-    shifts_ref, step_ref, level_ref, offsets_ref, image_hbm, sens_hbm, kspace_hbm, table_hbm,
-    landed,
-    image_ref, sens_ref, kspace_ref, parts_ref, table_ref, load_sem,
-    wrapped, rolled, gathered, entries, inverse, finished,
-    send_out, recv_out, send_back, recv_back, own_out, own_back,
+    step_ref, level_ref, shifts_hbm, offsets_hbm, image_hbm, sens_hbm, kspace_hbm, table_hbm,
+    out_ref,
+    shifts_ref, offsets_ref, image_ref, sens_ref, kspace_ref, parts_ref, table_ref, load_sem,
+    wrapped, rolled, gathered, entries, inverse, finished, landed,
+    send_out, recv_out, send_back, recv_back,
 ):
     total = frames * group
     plane_me = lax.axis_index("plane")
@@ -313,17 +354,19 @@
     base = plane_me - part_me
     me = frame_me * group + part_me
     rows = PATCH_Y
-
-    def flip(index, mask, count):
-        bit = 1
-        while bit < count:
-            if mask & bit:
-                index = index + bit - 2 * bit * lax.rem(index // bit, 2)
-            bit *= 2
-        return index
-
-    def device(index):
-        return {"plane": base + lax.rem(index, group), "frame": index // group}
+    everyone = [(f, q) for f in range(frames) for q in range(group)]
+
+    def other(f, q):
+        return (frame_me != f) | (part_me != q)
+
+    barrier = pltpu.get_barrier_semaphore()
+    for f, q in everyone:
+
+        @pl.when(other(f, q))
+        def _():
+            pl.semaphore_signal(
+                barrier, inc=1, device_id={"plane": base + q, "frame": f}, device_id_type=pl.DeviceIdType.MESH
+            )
 
     loads = {}
 
@@ -331,36 +374,63 @@
         loads[name] = pltpu.make_async_copy(source, target, load_sem.at[len(loads)])
         loads[name].start()
 
-    def load_plane(p):
+    load("offsets", offsets_hbm, offsets_ref)
+    load("table", table_hbm, parts_ref)
+    for p in range(planes):
+        load(("kspace", p), kspace_hbm.at[:, p], kspace_ref.at[:, p])
         load(("image", p), image_hbm.at[p], image_ref.at[p])
         load(("sens", p), sens_hbm.at[:, p], sens_ref.at[:, p])
-        load(("kspace", p), kspace_hbm.at[:, p], kspace_ref.at[:, p])
-
-    def start_later():
-        for p in range(1, planes):
-            load_plane(p)
-
-    load("table", table_hbm, parts_ref)
-    load_plane(0)
-
-    barrier = pltpu.get_barrier_semaphore()
-    for k in range(1, total):
-        pl.semaphore_signal(barrier, inc=1, device_id=device(flip(me, k, total)), device_id_type=pl.DeviceIdType.MESH)
-
-    lane = lax.broadcasted_iota(jnp.int32, (width_y, width_z), 1)
-    row = lax.broadcasted_iota(jnp.int32, (width_y, width_z), 0)
-    offset = jnp.broadcast_to(offsets_ref[...].astype(jnp.float32), (width_z, width_y)).T
-    wanted = jnp.where(offset == 0.0, 0.0, ACCEL - offset)
-    regular = lax.rem(lane, ACCEL).astype(jnp.float32) == wanted
-    low_y = (row < CENTER) | (row >= width_y - CENTER)
-    low_z = (lane < CENTER) | (lane >= width_z - CENTER)
-    sampled = (regular | (low_y & low_z)).astype(jnp.float32)
-
-    sends = []
+    load("shifts", shifts_hbm, shifts_ref)
+
+    loads["offsets"].wait()
+    patterns = row_patterns(offsets_ref, None, width_y, width_z)
     loads["table"].wait()
     lay_tables(parts_ref, table_ref, width_y)
+
+    half, quarter = frames // 2, frames // 4
+    far = frame_me // half
+    near = 1 - far
+    step_in = lax.rem(frame_me // quarter, 2)
+    inner = lax.rem(frame_me, quarter)
+
+    def order_out(p):
+        if ORDERS[p] == "near":
+            pairs_z = [(near, far, False), (far, near, True), (near, near, False), (far, far, True)]
+        elif ORDERS[p] == "xor":
+            pairs_z = [(near, 1 - step_in, False), (near, step_in, False), (far, 1 - step_in, False), (far, step_in, True)]
+        elif ORDERS[p] == "xorn":
+            pairs_z = [(near, step_in, False), (near, 1 - step_in, False), (far, 1 - step_in, False), (far, step_in, True)]
+        elif ORDERS[p] == "cross":
+            pairs_z = [(near, far, False), (near, near, False), (far, near, True), (far, far, True)]
+        for z_high, z_low, maybe in pairs_z:
+            for k in reversed(range(quarter)):
+                x = lax.rem(inner + k, quarter)
+                for r in reversed(range(group)):
+                    q = lax.rem(part_me + r, group)
+                    yield z_high * half + z_low * quarter + x, q, maybe and k == 0 and r == 0
+
+    def send(p, f, q, maybe):
+        block = rolled.at[p, :, pl.ds(pl.multiple_of((f * group + q) * rows, rows), rows), :]
+        copy = pltpu.make_async_remote_copy(
+            src_ref=block,
+            dst_ref=gathered.at[p, part_me, frame_me],
+            send_sem=send_out.at[p, f, q],
+            recv_sem=recv_out.at[p, frame_me, part_me],
+            device_id={"plane": base + q, "frame": f},
+            device_id_type=pl.DeviceIdType.MESH,
+        )
+        apart = other(f, q) if maybe else None
+        if maybe:
+            pl.when(apart)(copy.start)
+        else:
+            copy.start()
+        return apart, copy
+
+    sends = []
     for p in range(planes):
-        moved = moved_plane(loads, start_later, p, coils, width_y, image_ref, sens_ref, kspace_ref, table_ref, step_ref[0], sampled)
+        moved = moved_plane(loads, p, coils, width_y, image_ref, sens_ref, kspace_ref, table_ref, step_ref[0], patterns)
+        if p == 0:
+            loads["shifts"].wait()
         for k in range(2):
             part = pltpu.roll(moved[k], shifts_ref[1], 1)
             wrapped[p, k, pl.ds(0, rows), :] = part[width_y - rows :]
@@ -368,33 +438,19 @@
             rolled[p, k] = wrapped[p, k, pl.ds(rows - shifts_ref[0], width_y), :]
         if p == 0:
             pl.semaphore_wait(barrier, total - 1)
-        group_sends = []
-        for k in reversed(range(1, total)):
-            target = flip(me, k, total)
-            copy = pltpu.make_async_remote_copy(
-                src_ref=rolled.at[p, :, pl.ds(pl.multiple_of(target * rows, rows), rows), :],
-                dst_ref=gathered.at[p, part_me, frame_me],
-                send_sem=send_out.at[p, k],
-                recv_sem=recv_out.at[p, k],
-                device_id=device(target),
-                device_id_type=pl.DeviceIdType.MESH,
-            )
-            copy.start()
-            group_sends.append(copy)
-        own = pltpu.make_async_copy(
+        pltpu.make_async_copy(
             rolled.at[p, :, pl.ds(pl.multiple_of(me * rows, rows), rows), :],
             gathered.at[p, part_me, frame_me],
-            own_out.at[p],
-        )
-        own.start()
-        sends.append((group_sends, own))
+            recv_out.at[p, frame_me, part_me],
+        ).start()
+        for f, q, maybe in order_out(p):
+            sends.append(send(p, f, q, maybe))
 
     pairs = [(f, g) for f in range(frames) for g in range(f + 1)]
     for p in range(planes):
-        group_sends, own = sends[p]
-        own.wait()
-        for copy in group_sends:
-            copy.wait_recv()
+        for f, q in everyone:
+            place = gathered.at[p, q, f]
+            pltpu.make_async_copy(place, place, recv_out.at[p, f, q]).wait()
         for n, (f, g) in enumerate(pairs):
             sum_re = None
             sum_im = None
@@ -456,45 +512,36 @@
                     im = im + (w_re * g_im + w_im * g_re)
                 finished[q, f, p, 0] = re
                 finished[q, f, p, 1] = im
-            mine = (frame_me == f) & (part_me == q)
-            local = pltpu.make_async_copy(finished.at[q, f], landed.at[:, 0, :, spot, :], own_back)
+            place = landed.at[:, :, spot, :]
+            apart = other(f, q)
             copy = pltpu.make_async_remote_copy(
                 src_ref=finished.at[q, f],
-                dst_ref=landed.at[:, 0, :, spot, :],
-                send_sem=send_back.at[q, f],
-                recv_sem=recv_back.at[part_me, frame_me],
+                dst_ref=place,
+                send_sem=send_back.at[f, q],
+                recv_sem=recv_back.at[frame_me, part_me],
                 device_id={"plane": base + q, "frame": f},
                 device_id_type=pl.DeviceIdType.MESH,
             )
-            pl.when(mine)(local.start)
-            pl.when(jnp.logical_not(mine))(copy.start)
-            backs.append((mine, copy))
-    local.wait()
-    for f in range(frames):
-        for q in range(group):
-            other = jnp.logical_not((frame_me == f) & (part_me == q))
-            copy = pltpu.make_async_remote_copy(
-                src_ref=finished.at[q, f],
-                dst_ref=landed.at[:, 0, :, pl.ds((f * group + q) * rows, rows), :],
-                send_sem=send_back.at[q, f],
-                recv_sem=recv_back.at[q, f],
-                device_id={"plane": base + q, "frame": f},
-                device_id_type=pl.DeviceIdType.MESH,
-            )
-            pl.when(other)(copy.wait)
-    for group_sends, own in sends:
-        for copy in group_sends:
+            pl.when(apart)(copy.start)
+            pl.when(jnp.logical_not(apart))(pltpu.make_async_copy(finished.at[q, f], place, recv_back.at[f, q]).start)
+            backs.append((apart, copy))
+    for apart, copy in sends:
+        if apart is None:
             copy.wait_send()
-
-
-def unroll_kernel(planes, width_y, width_z, shifts_ref, landed_ref, out_ref, wrapped):
+        else:
+            pl.when(apart)(copy.wait_send)
+    for f, q in everyone:
+        place = landed.at[:, :, pl.ds((f * group + q) * rows, rows), :]
+        pltpu.make_async_copy(place, place, recv_back.at[f, q]).wait()
     shift_z = lax.rem(width_z - shifts_ref[1], width_z)
     for p in range(planes):
         for k in range(2):
-            part = pltpu.roll(landed_ref[p, 0, k], shift_z, 1)
+            part = pltpu.roll(landed[p, k], shift_z, 1)
             wrapped[p, k, pl.ds(0, width_y), :] = part
-            wrapped[p, k, pl.ds(width_y, PATCH_Y), :] = part[:PATCH_Y]
+            wrapped[p, k, pl.ds(width_y, rows), :] = part[:rows]
             out_ref[p, 0, k] = wrapped[p, k, pl.ds(shifts_ref[0], width_y), :]
+    for apart, copy in backs:
+        pl.when(apart)(copy.wait_send)
 
 
 def local_fused(image, sens, kspace, offsets, shifts, step_size, threshold):
@@ -509,44 +556,38 @@
     hbm = pl.BlockSpec(memory_space=pltpu.HBM)
     slab = (PATCH_Y, width_z)
     dma = pltpu.SemaphoreType.DMA
-    image, sens, kspace, table = [pltpu.with_memory_space_constraint(x, pltpu.HBM) for x in (image, sens, kspace, table)]
-    landed = pl.pallas_call(
+    in_hbm = [
+        pltpu.with_memory_space_constraint(x, pltpu.HBM) for x in (shifts, offsets, image, sens, kspace, table)
+    ]
+    return pl.pallas_call(
         functools.partial(step_kernel, planes, frames, group, coils, width_y, width_z),
         out_shape=jax.ShapeDtypeStruct(image.shape, jnp.float32),
-        in_specs=[smem, smem, smem, vmem, hbm, hbm, hbm, hbm],
-        out_specs=pl.BlockSpec(memory_space=pl.ANY),
+        in_specs=[smem, smem] + [hbm] * 6,
+        out_specs=vmem,
         scratch_shapes=[
+            pltpu.SMEM(shifts.shape, shifts.dtype),
+            pltpu.VMEM(offsets.shape, offsets.dtype),
             pltpu.VMEM(image.shape, image.dtype),
             pltpu.VMEM(sens.shape, sens.dtype),
             pltpu.VMEM(kspace.shape, kspace.dtype),
             pltpu.VMEM(table.shape, table.dtype),
             pltpu.VMEM((4, 2 * width_y, 2 * width_y), table.dtype),
-            dma((3 * planes + 1,)),
+            dma((3 * planes + 3,)),
             pltpu.VMEM((planes, 2, width_y + PATCH_Y, width_z), jnp.float32),
             pltpu.VMEM((planes, 2, width_y, width_z), jnp.float32),
             pltpu.VMEM((planes, group, frames, 2) + slab, jnp.float32),
             pltpu.VMEM((frames * frames,) + slab, jnp.float32),
             pltpu.VMEM((frames, frames, 2) + slab, jnp.float32),
             pltpu.VMEM((group, frames, planes, 2) + slab, jnp.float32),
-            dma((planes, total)),
-            dma((planes, total)),
-            dma((group, frames)),
-            dma((group, frames)),
-            dma((planes,)),
-            dma(()),
+            pltpu.VMEM((planes, 2, width_y, width_z), jnp.float32),
+            dma((planes, frames, group)),
+            dma((planes, frames, group)),
+            dma((frames, group)),
+            dma((frames, group)),
         ],
         compiler_params=pltpu.CompilerParams(collective_id=0, has_side_effects=True, vmem_limit_bytes=VMEM_BYTES),
         name="prox_step",
-    )(shifts, step_size, threshold, offsets, image, sens, kspace, table)
-    return pl.pallas_call(
-        functools.partial(unroll_kernel, planes, width_y, width_z),
-        out_shape=jax.ShapeDtypeStruct(image.shape, jnp.float32),
-        in_specs=[smem, vmem],
-        out_specs=vmem,
-        scratch_shapes=[pltpu.VMEM((planes, 2, width_y + PATCH_Y, width_z), jnp.float32)],
-        compiler_params=pltpu.CompilerParams(vmem_limit_bytes=VMEM_BYTES),
-        name="shift_back",
-    )(shifts, landed)
+    )(step_size, threshold, *in_hbm)
 
 
 def local(image, sens, kspace, offsets, shifts, step_size, threshold):

time: 23.8 us -> 22.5 us (0.945)
  Pallas kernels: 22.3 us -> 20.3 us
  local copies, waits for them, and re-layouts: 0.01 us -> 0.71 us
    pallas_call x1 -> x0, Pallas kernels: 1.39 us -> none  [local_fused(): pl.pallas_call(functools.partial(unroll_kernel, planes, width_y, width_z)...]
    unnamed x4 -> x1, local copies, waits for them, and re-layouts: 0.01 us -> 0.71 us
    pallas_call x1, Pallas kernels: 20.9 us -> 20.3 us  [local_fused(): pl.pallas_call(functools.partial(step_kernel, planes, frames, group, coil...]
where the time goes in v2:
time: 22.5 us; the launch traced here: 22.3 us
  Pallas kernels  20.3 us (90%)
  between operations  1.3 us (6%)
  local copies, waits for them, and re-layouts  0.71 us (3%)
    pallas_call x1, Pallas kernels, local_fused(): pl.pallas_call(functools.partial(step_kernel, planes, frames, group, coil...  20.3 us
    unnamed x1, local copies, waits for them, and re-layouts  0.71 us

profile of v2, /device:TPU:0, one launch (start us, length us, event | category | flops | bytes accessed | tf_op | source)
XLA Modules:
  0.0 22.3 jit_solution(3584816718499805364)
XLA Ops:
  1.3 20.3 %prox_step.1 = f32[2,1,2,128,128]{4,3,2,1,0:T(8,128)S(1)} custom-call(f32[1]{0:T(128)S(6)} %copy.10.step_ref, f32[1]{0:T(128)S(6)} %copy.11.level_ref, s32[2]{0:T(128)} %shifts_hbm.1, s32[1,128]{1,0:T(1,128)} %offsets_hbm.1, f32[2,1,2,128,128]{4,3,2,1,0:T(8,128)} %image_hbm.1, bf16[4,2,2,128,128]{4,3,2,1,0:T(8,128)(2,1)} %sens_hbm.1, ...), custom_call_target="tpu_custom_call" | custom-call | tf_op jit(solution)/shard_map/prox_step/pallas_call | solution.py:562
  21.6 0.7 %copy.12 = f32[2,1,2,128,128]{4,3,2,1,0:T(8,128)} copy(f32[2,1,2,128,128]{4,3,2,1,0:T(8,128)S(1)} %prox_step.1) | data formatting | bytes 524288

commit v3 on v2

--- a/solution.py
+++ b/solution.py
@@ -168,7 +168,12 @@
 VMEM_BYTES = 24 * 1024 * 1024
 
 
-ORDERS = ('near', 'near')
+PLAN = [[(0, 'a'), (0, 'c'), (0, 'b'), (0, 'd')], [(1, 'a'), (1, 'c'), (1, 'b'), (1, 'd')]]
+
+
+def two_parts(table):
+    high = table.astype(jnp.bfloat16)
+    return high, (table - high.astype(np.float64)).astype(jnp.bfloat16)
 
 
 def block_tables(length):
@@ -176,22 +181,28 @@
     angles = (indices[:, None] * indices[None, :] % length) * (2.0 * np.pi / length)
     cos = np.cos(angles) / np.sqrt(length)
     sin = np.sin(angles) / np.sqrt(length)
-    parts = []
-    for table in (cos, sin):
-        high = table.astype(jnp.bfloat16)
-        parts += [high, (table - high.astype(np.float64)).astype(jnp.bfloat16)]
-    return np.stack(parts)
+    centre = np.concatenate([indices[:CENTER], indices[length - CENTER :]])
+    into = np.block([[cos, -sin], [sin, cos]])[:, np.concatenate([centre, length + centre])]
+    into_high, into_low = two_parts(into)
+    from_high, from_low = two_parts(into.T)
+    rest = length - 4 * len(centre)
+    into = np.concatenate([into_high, into_low, np.zeros((2 * length, rest), jnp.bfloat16)], axis=1)
+    rest = length - 6 * len(centre)
+    back = np.concatenate([from_high, from_low, from_high, np.zeros((rest, 2 * length), jnp.bfloat16)], axis=0)
+    whole = np.concatenate([*two_parts(cos), *two_parts(sin)], axis=0)
+    return np.concatenate([whole, into, back[:, :length], back[:, length:]], axis=0)
 
 
 def lay_tables(parts_ref, table_ref, width):
     low, top = pl.ds(0, width), pl.ds(width, width)
     for k in range(2):
-        cos, sin = parts_ref[k], parts_ref[2 + k]
-        for table, upper, lower in ((k, sin, -sin), (2 + k, -sin, sin)):
-            table_ref[table, low, low] = cos
-            table_ref[table, top, top] = cos
-            table_ref[table, low, top] = upper
-            table_ref[table, top, low] = lower
+        cos, sin = parts_ref[pl.ds(k * width, width)], parts_ref[pl.ds((2 + k) * width, width)]
+        for table, upper, lower in ((0, sin, -sin), (1, -sin, sin)):
+            first, second = pl.ds(2 * k * width, width), pl.ds((2 * k + 1) * width, width)
+            table_ref[table, first, low] = cos
+            table_ref[table, second, top] = cos
+            table_ref[table, first, top] = upper
+            table_ref[table, second, low] = lower
 
 
 def halves(values):
@@ -203,14 +214,11 @@
     return jnp.dot(left, right, preferred_element_type=jnp.float32)
 
 
-def from_right(values, high, low):
+def from_left(table, values):
+    count = table.shape[1]
     value_high, value_low = halves(values)
-    return mul(value_high, high) + mul(value_high, low) + mul(value_low, high)
-
-
-def from_left(high, low, values):
-    value_high, value_low = halves(values)
-    return mul(high, value_high) + mul(low, value_high) + mul(high, value_low)
+    first = mul(table, value_high)
+    return first[:count] + (first[count:] + mul(table[:count], value_low))
 
 
 def row_patterns(offsets_ref, offset_rows, width_y, width_z):
@@ -226,13 +234,16 @@
     kept = jnp.where(regular | centre, scale, 0.0).astype(jnp.bfloat16)
     extra = jnp.where(centre & jnp.logical_not(regular), scale, 0.0)
     edge = jnp.concatenate([extra[:CENTER], extra[width_y - CENTER :]], axis=0)
+    edge = jnp.where(lane[: 2 * CENTER] < CENTER, edge, pltpu.roll(edge, 2 * CENTER, 1))
+    slot = lane[: 2 * CENTER]
+    edge = jnp.where(slot < 2 * CENTER, edge, jnp.where(slot < 4 * CENTER, pltpu.roll(edge, 2 * CENTER, 1), 0.0))
     half = jnp.where((offset == 0.0) | (offset == 2.0), 1.0, -1.0)
     real = jnp.where(offset == 0.0, 1.0, jnp.where(offset == 2.0, -1.0, 0.0))
     imag = jnp.where(offset == 1.0, -1.0, jnp.where(offset == 3.0, 1.0, 0.0))
     return kept, edge, half, real, imag
 
 
-def moved_plane(loads, p, coils, width, image_ref, sens_ref, kspace_ref, table_ref, step, patterns):
+def moved_plane(loads, start_later, p, coils, width, image_ref, sens_ref, kspace_ref, parts_ref, table_ref, step, patterns):
     kept, edge, half, real, imag = patterns
     loads["kspace", p].wait()
     data = jnp.concatenate(
@@ -242,9 +253,11 @@
         ],
         axis=0,
     )
-    known = mul(data, table_ref[0]) + mul(data, table_ref[1])
+    known = mul(data, table_ref[0, : 2 * width]) + mul(data, table_ref[0, 2 * width :])
     loads["image", p].wait()
     loads["sens", p].wait()
+    if p == 0:
+        start_later()
     image_re = image_ref[p, 0, 0]
     image_im = image_ref[p, 0, 1]
     coil_re, coil_im = [], []
@@ -254,7 +267,7 @@
         coil_re.append(sens_re * image_re - sens_im * image_im)
         coil_im.append(sens_re * image_im + sens_im * image_re)
     stacked = jnp.concatenate([jnp.concatenate(coil_re, axis=1), jnp.concatenate(coil_im, axis=1)], axis=0)
-    lines = from_left(table_ref[0], table_ref[1], stacked)
+    lines = from_left(table_ref[0], stacked)
 
     def part(k, c):
         return lines[k * width : (k + 1) * width, c * width : (c + 1) * width]
@@ -268,8 +281,15 @@
         ],
         axis=0,
     )
-    weight = jnp.concatenate([jnp.concatenate([edge] * 2, axis=1)] * coils, axis=0)
-    added = from_right(weight * from_right(low, table_ref[2], table_ref[3]), table_ref[0], table_ref[1])
+    weight = jnp.concatenate([edge] * coils, axis=0)
+    into = parts_ref[pl.ds(4 * width, 2 * width)]
+    out = jnp.concatenate([parts_ref[pl.ds(6 * width, width)], parts_ref[pl.ds(7 * width, width)]], axis=1)
+    found = mul(jnp.concatenate(halves(low), axis=0), into)
+    found = found[: low.shape[0]] + found[low.shape[0] :]
+    found = weight * (found + pltpu.roll(found, width - 4 * CENTER, 1))
+    found_high = found.astype(jnp.bfloat16).astype(jnp.float32)
+    three = found_high + pltpu.roll(found_high, 4 * CENTER, 1) + pltpu.roll(found - found_high, 8 * CENTER, 1)
+    added = mul(three.astype(jnp.bfloat16), out)
     resid_re, resid_im = [], []
     for c in range(coils):
         both = []
@@ -295,7 +315,7 @@
                 )
             )
     resid = jnp.concatenate([jnp.concatenate(resid_re, axis=1), jnp.concatenate(resid_im, axis=1)], axis=0)
-    back = from_left(table_ref[2], table_ref[3], resid)
+    back = from_left(table_ref[1], resid)
     grad_re = jnp.zeros_like(image_re)
     grad_im = jnp.zeros_like(image_im)
     for c in range(coils):
@@ -376,11 +396,18 @@
 
     load("offsets", offsets_hbm, offsets_ref)
     load("table", table_hbm, parts_ref)
-    for p in range(planes):
+
+    def load_plane(p):
         load(("kspace", p), kspace_hbm.at[:, p], kspace_ref.at[:, p])
         load(("image", p), image_hbm.at[p], image_ref.at[p])
         load(("sens", p), sens_hbm.at[:, p], sens_ref.at[:, p])
+
+    load_plane(0)
     load("shifts", shifts_hbm, shifts_ref)
+
+    def start_later():
+        for p in range(1, planes):
+            load_plane(p)
 
     loads["offsets"].wait()
     patterns = row_patterns(offsets_ref, None, width_y, width_z)
@@ -393,42 +420,41 @@
     step_in = lax.rem(frame_me // quarter, 2)
     inner = lax.rem(frame_me, quarter)
 
-    def order_out(p):
-        if ORDERS[p] == "near":
-            pairs_z = [(near, far, False), (far, near, True), (near, near, False), (far, far, True)]
-        elif ORDERS[p] == "xor":
-            pairs_z = [(near, 1 - step_in, False), (near, step_in, False), (far, 1 - step_in, False), (far, step_in, True)]
-        elif ORDERS[p] == "xorn":
-            pairs_z = [(near, step_in, False), (near, 1 - step_in, False), (far, 1 - step_in, False), (far, step_in, True)]
-        elif ORDERS[p] == "cross":
-            pairs_z = [(near, far, False), (near, near, False), (far, near, True), (far, far, True)]
-        for z_high, z_low, maybe in pairs_z:
-            for k in reversed(range(quarter)):
-                x = lax.rem(inner + k, quarter)
-                for r in reversed(range(group)):
-                    q = lax.rem(part_me + r, group)
-                    yield z_high * half + z_low * quarter + x, q, maybe and k == 0 and r == 0
+    def order_out(token):
+        zone, only = token[0], token[1:]
+        z_high, z_low, maybe = {
+            "a": (near, far, False), "b": (near, near, False), "c": (far, near, True), "d": (far, far, True),
+            "3": (near, 1 - step_in, False), "2": (near, step_in, False), "1": (far, 1 - step_in, False), "0": (far, step_in, True),
+        }[zone]
+        for k in reversed(range(quarter)):
+            x = lax.rem(inner + k, quarter)
+            if only in ("0", "1"):
+                yield z_high * half + z_low * quarter + x, int(only), maybe and k == 0
+                continue
+            for r in reversed(range(group)):
+                q = lax.rem(part_me + r, group)
+                yield z_high * half + z_low * quarter + x, q, maybe and k == 0 and r == 0
 
     def send(p, f, q, maybe):
         block = rolled.at[p, :, pl.ds(pl.multiple_of((f * group + q) * rows, rows), rows), :]
         copy = pltpu.make_async_remote_copy(
             src_ref=block,
             dst_ref=gathered.at[p, part_me, frame_me],
-            send_sem=send_out.at[p, f, q],
-            recv_sem=recv_out.at[p, frame_me, part_me],
+            send_sem=send_out.at[p],
+            recv_sem=recv_out.at[p],
             device_id={"plane": base + q, "frame": f},
             device_id_type=pl.DeviceIdType.MESH,
         )
-        apart = other(f, q) if maybe else None
         if maybe:
-            pl.when(apart)(copy.start)
+            pl.when(other(f, q))(copy.start)
         else:
             copy.start()
-        return apart, copy
-
-    sends = []
+
+    def landed_all(ref, sem):
+        pltpu.make_async_copy(ref, ref, sem).wait()
+
     for p in range(planes):
-        moved = moved_plane(loads, p, coils, width_y, image_ref, sens_ref, kspace_ref, table_ref, step_ref[0], patterns)
+        moved = moved_plane(loads, start_later, p, coils, width_y, image_ref, sens_ref, kspace_ref, parts_ref, table_ref, step_ref[0], patterns)
         if p == 0:
             loads["shifts"].wait()
         for k in range(2):
@@ -441,16 +467,15 @@
         pltpu.make_async_copy(
             rolled.at[p, :, pl.ds(pl.multiple_of(me * rows, rows), rows), :],
             gathered.at[p, part_me, frame_me],
-            recv_out.at[p, frame_me, part_me],
+            recv_out.at[p],
         ).start()
-        for f, q, maybe in order_out(p):
-            sends.append(send(p, f, q, maybe))
+        for wp, zone in PLAN[p]:
+            for f, q, maybe in order_out(zone):
+                send(wp, f, q, maybe)
 
     pairs = [(f, g) for f in range(frames) for g in range(f + 1)]
     for p in range(planes):
-        for f, q in everyone:
-            place = gathered.at[p, q, f]
-            pltpu.make_async_copy(place, place, recv_out.at[p, f, q]).wait()
+        landed_all(gathered.at[p], recv_out.at[p])
         for n, (f, g) in enumerate(pairs):
             sum_re = None
             sum_im = None
@@ -497,7 +522,6 @@
         else:
             inverse[f, f, 1] = jnp.zeros_like(re)
 
-    backs = []
     spot = pl.ds(pl.multiple_of(me * rows, rows), rows)
     for f in range(frames):
         weights = [(inverse[f, g, 0], inverse[f, g, 1]) for g in range(frames)]
@@ -517,22 +541,17 @@
             copy = pltpu.make_async_remote_copy(
                 src_ref=finished.at[q, f],
                 dst_ref=place,
-                send_sem=send_back.at[f, q],
-                recv_sem=recv_back.at[frame_me, part_me],
+                send_sem=send_back,
+                recv_sem=recv_back,
                 device_id={"plane": base + q, "frame": f},
                 device_id_type=pl.DeviceIdType.MESH,
             )
             pl.when(apart)(copy.start)
-            pl.when(jnp.logical_not(apart))(pltpu.make_async_copy(finished.at[q, f], place, recv_back.at[f, q]).start)
-            backs.append((apart, copy))
-    for apart, copy in sends:
-        if apart is None:
-            copy.wait_send()
-        else:
-            pl.when(apart)(copy.wait_send)
-    for f, q in everyone:
-        place = landed.at[:, :, pl.ds((f * group + q) * rows, rows), :]
-        pltpu.make_async_copy(place, place, recv_back.at[f, q]).wait()
+            pl.when(jnp.logical_not(apart))(pltpu.make_async_copy(finished.at[q, f], place, recv_back).start)
+    sent = pl.ds(0, (total - 1) * rows)
+    for p in range(planes):
+        landed_all(rolled.at[p, :, sent, :], send_out.at[p])
+    landed_all(landed, recv_back)
     shift_z = lax.rem(width_z - shifts_ref[1], width_z)
     for p in range(planes):
         for k in range(2):
@@ -540,8 +559,7 @@
             wrapped[p, k, pl.ds(0, width_y), :] = part
             wrapped[p, k, pl.ds(width_y, rows), :] = part[:rows]
             out_ref[p, 0, k] = wrapped[p, k, pl.ds(shifts_ref[0], width_y), :]
-    for apart, copy in backs:
-        pl.when(apart)(copy.wait_send)
+    landed_all(landed.at[:, :, sent, :], send_back)
 
 
 def local_fused(image, sens, kspace, offsets, shifts, step_size, threshold):
@@ -571,7 +589,7 @@
             pltpu.VMEM(sens.shape, sens.dtype),
             pltpu.VMEM(kspace.shape, kspace.dtype),
             pltpu.VMEM(table.shape, table.dtype),
-            pltpu.VMEM((4, 2 * width_y, 2 * width_y), table.dtype),
+            pltpu.VMEM((2, 4 * width_y, 2 * width_y), table.dtype),
             dma((3 * planes + 3,)),
             pltpu.VMEM((planes, 2, width_y + PATCH_Y, width_z), jnp.float32),
             pltpu.VMEM((planes, 2, width_y, width_z), jnp.float32),
@@ -580,10 +598,10 @@
             pltpu.VMEM((frames, frames, 2) + slab, jnp.float32),
             pltpu.VMEM((group, frames, planes, 2) + slab, jnp.float32),
             pltpu.VMEM((planes, 2, width_y, width_z), jnp.float32),
-            dma((planes, frames, group)),
-            dma((planes, frames, group)),
-            dma((frames, group)),
-            dma((frames, group)),
+            dma((planes,)),
+            dma((planes,)),
+            dma(()),
+            dma(()),
         ],
         compiler_params=pltpu.CompilerParams(collective_id=0, has_side_effects=True, vmem_limit_bytes=VMEM_BYTES),
         name="prox_step",

time: 22.5 us -> 21.7 us (0.964)
  Pallas kernels: 20.3 us -> 19.5 us
    pallas_call x1, Pallas kernels: 20.3 us -> 19.5 us  [local_fused(): pl.pallas_call(functools.partial(step_kernel, planes, frames, group, coil...]
where the time goes in v3:
time: 21.7 us; the launch traced here: 21.5 us
  Pallas kernels  19.5 us (90%)
  between operations  1.3 us (6%)
  local copies, waits for them, and re-layouts  0.71 us (3%)
    pallas_call x1, Pallas kernels, local_fused(): pl.pallas_call(functools.partial(step_kernel, planes, frames, group, coil...  19.5 us
    unnamed x1, local copies, waits for them, and re-layouts  0.71 us

profile of v3, /device:TPU:0, one launch (start us, length us, event | category | flops | bytes accessed | tf_op | source)
XLA Modules:
  0.0 21.5 jit_solution(16470449921139118962)
XLA Ops:
  1.3 19.5 %prox_step.1 = f32[2,1,2,128,128]{4,3,2,1,0:T(8,128)S(1)} custom-call(f32[1]{0:T(128)S(6)} %copy.10.step_ref, f32[1]{0:T(128)S(6)} %copy.11.level_ref, s32[2]{0:T(128)} %shifts_hbm.1, s32[1,128]{1,0:T(1,128)} %offsets_hbm.1, f32[2,1,2,128,128]{4,3,2,1,0:T(8,128)} %image_hbm.1, bf16[4,2,2,128,128]{4,3,2,1,0:T(8,128)(2,1)} %sens_hbm.1, ...), custom_call_target="tpu_custom_call" | custom-call | tf_op jit(solution)/shard_map/prox_step/pallas_call | solution.py:580
  20.8 0.7 %copy.12 = f32[2,1,2,128,128]{4,3,2,1,0:T(8,128)} copy(f32[2,1,2,128,128]{4,3,2,1,0:T(8,128)S(1)} %prox_step.1) | data formatting | bytes 524288

commit v4 on v3

--- a/solution.py
+++ b/solution.py
@@ -14,6 +14,7 @@
 PATCH_Z = 8
 ACCEL = 4
 CENTER = 8
+PAIR = 2
 
 
 def from_partner(block, axis, distance):
@@ -168,7 +169,7 @@
 VMEM_BYTES = 24 * 1024 * 1024
 
 
-PLAN = [[(0, 'a'), (0, 'c'), (0, 'b'), (0, 'd')], [(1, 'a'), (1, 'c'), (1, 'b'), (1, 'd')]]
+PLAN = [[(0, 'W'), (0, 'Y'), (0, 'X'), (0, 'Z')], [(1, 'W'), (1, 'Y'), (1, 'X'), (1, 'Z')]]
 
 
 def two_parts(table):
@@ -245,86 +246,90 @@
 
 def moved_plane(loads, start_later, p, coils, width, image_ref, sens_ref, kspace_ref, parts_ref, table_ref, step, patterns):
     kept, edge, half, real, imag = patterns
+    sides = [range(c, min(c + PAIR, coils)) for c in range(0, coils, PAIR)]
     loads["kspace", p].wait()
-    data = jnp.concatenate(
-        [
-            jnp.concatenate([kspace_ref[c, p, 0, k] * kept for k in range(2)], axis=1)
-            for c in range(coils)
-        ],
-        axis=0,
-    )
-    known = mul(data, table_ref[0, : 2 * width]) + mul(data, table_ref[0, 2 * width :])
+    known = []
+    for side in sides:
+        data = jnp.concatenate(
+            [jnp.concatenate([kspace_ref[c, p, 0, k] * kept for k in range(2)], axis=1) for c in side], axis=0
+        )
+        known.append(mul(data, table_ref[0, : 2 * width]) + mul(data, table_ref[0, 2 * width :]))
     loads["image", p].wait()
     loads["sens", p].wait()
     if p == 0:
         start_later()
     image_re = image_ref[p, 0, 0]
     image_im = image_ref[p, 0, 1]
-    coil_re, coil_im = [], []
-    for c in range(coils):
-        sens_re = sens_ref[c, p, 0].astype(jnp.float32)
-        sens_im = sens_ref[c, p, 1].astype(jnp.float32)
-        coil_re.append(sens_re * image_re - sens_im * image_im)
-        coil_im.append(sens_re * image_im + sens_im * image_re)
-    stacked = jnp.concatenate([jnp.concatenate(coil_re, axis=1), jnp.concatenate(coil_im, axis=1)], axis=0)
-    lines = from_left(table_ref[0], stacked)
-
-    def part(k, c):
-        return lines[k * width : (k + 1) * width, c * width : (c + 1) * width]
-
-    low = jnp.concatenate(
-        [
-            jnp.concatenate(
-                [jnp.concatenate([part(k, c)[:CENTER], part(k, c)[width - CENTER :]], axis=0) for k in range(2)], axis=1
-            )
-            for c in range(coils)
-        ],
-        axis=0,
-    )
-    weight = jnp.concatenate([edge] * coils, axis=0)
+
+    def sens(c):
+        return sens_ref[c, p, 0].astype(jnp.float32), sens_ref[c, p, 1].astype(jnp.float32)
+
+    lines = []
+    for side in sides:
+        coil_re, coil_im = [], []
+        for c in side:
+            sens_re, sens_im = sens(c)
+            coil_re.append(sens_re * image_re - sens_im * image_im)
+            coil_im.append(sens_re * image_im + sens_im * image_re)
+        stacked = jnp.concatenate([jnp.concatenate(coil_re, axis=1), jnp.concatenate(coil_im, axis=1)], axis=0)
+        lines.append(from_left(table_ref[0], stacked))
     into = parts_ref[pl.ds(4 * width, 2 * width)]
     out = jnp.concatenate([parts_ref[pl.ds(6 * width, width)], parts_ref[pl.ds(7 * width, width)]], axis=1)
-    found = mul(jnp.concatenate(halves(low), axis=0), into)
-    found = found[: low.shape[0]] + found[low.shape[0] :]
-    found = weight * (found + pltpu.roll(found, width - 4 * CENTER, 1))
-    found_high = found.astype(jnp.bfloat16).astype(jnp.float32)
-    three = found_high + pltpu.roll(found_high, 4 * CENTER, 1) + pltpu.roll(found - found_high, 8 * CENTER, 1)
-    added = mul(three.astype(jnp.bfloat16), out)
-    resid_re, resid_im = [], []
-    for c in range(coils):
-        both = []
-        for k in range(2):
-            line = part(k, c)
-            both.append(line + half * pltpu.roll(line, width // 2, 1))
-        turned = [pltpu.roll(line, width // 4, 1) for line in both]
-        sums = [
-            both[0] + (real * turned[0] - imag * turned[1]),
-            both[1] + (real * turned[1] + imag * turned[0]),
-        ]
-        for k, out in ((0, resid_re), (1, resid_im)):
-            value = sums[k] - known[c * width : (c + 1) * width, k * width : (k + 1) * width]
-            more = added[2 * CENTER * c : 2 * CENTER * (c + 1), k * width : (k + 1) * width]
-            out.append(
-                jnp.concatenate(
-                    [
-                        value[:CENTER] + more[:CENTER],
-                        value[CENTER : width - CENTER],
-                        value[width - CENTER :] + more[CENTER:],
-                    ],
-                    axis=0,
-                )
-            )
-    resid = jnp.concatenate([jnp.concatenate(resid_re, axis=1), jnp.concatenate(resid_im, axis=1)], axis=0)
-    back = from_left(table_ref[1], resid)
     grad_re = jnp.zeros_like(image_re)
     grad_im = jnp.zeros_like(image_im)
-    for c in range(coils):
-        back_re = back[:width, c * width : (c + 1) * width]
-        back_im = back[width:, c * width : (c + 1) * width]
-        sens_re = sens_ref[c, p, 0].astype(jnp.float32)
-        sens_im = sens_ref[c, p, 1].astype(jnp.float32)
-        grad_re += sens_re * back_re + sens_im * back_im
-        grad_im += sens_re * back_im - sens_im * back_re
+    for side, line, data in zip(sides, lines, known):
+        count = len(side)
+
+        def part(k, n):
+            return line[k * width : (k + 1) * width, n * width : (n + 1) * width]
+
+        low = jnp.concatenate(
+            [
+                jnp.concatenate(
+                    [jnp.concatenate([part(k, n)[:CENTER], part(k, n)[width - CENTER :]], axis=0) for k in range(2)],
+                    axis=1,
+                )
+                for n in range(count)
+            ],
+            axis=0,
+        )
+        weight = jnp.concatenate([edge] * count, axis=0)
+        found = mul(jnp.concatenate(halves(low), axis=0), into)
+        found = found[: low.shape[0]] + found[low.shape[0] :]
+        found = weight * (found + pltpu.roll(found, width - 4 * CENTER, 1))
+        found_high = found.astype(jnp.bfloat16).astype(jnp.float32)
+        three = found_high + pltpu.roll(found_high, 4 * CENTER, 1) + pltpu.roll(found - found_high, 8 * CENTER, 1)
+        added = mul(three.astype(jnp.bfloat16), out)
+        resid = ([], [])
+        for n in range(count):
+            both = []
+            for k in range(2):
+                both.append(part(k, n) + half * pltpu.roll(part(k, n), width // 2, 1))
+            turned = [pltpu.roll(value, width // 4, 1) for value in both]
+            sums = [
+                both[0] + (real * turned[0] - imag * turned[1]),
+                both[1] + (real * turned[1] + imag * turned[0]),
+            ]
+            for k in range(2):
+                value = sums[k] - data[n * width : (n + 1) * width, k * width : (k + 1) * width]
+                more = added[2 * CENTER * n : 2 * CENTER * (n + 1), k * width : (k + 1) * width]
+                resid[k].append(
+                    jnp.concatenate(
+                        [
+                            value[:CENTER] + more[:CENTER],
+                            value[CENTER : width - CENTER],
+                            value[width - CENTER :] + more[CENTER:],
+                        ],
+                        axis=0,
+                    )
+                )
+        back = from_left(table_ref[1], jnp.concatenate([jnp.concatenate(r, axis=1) for r in resid], axis=0))
+        for n, c in enumerate(side):
+            back_re = back[:width, n * width : (n + 1) * width]
+            back_im = back[width:, n * width : (n + 1) * width]
+            sens_re, sens_im = sens(c)
+            grad_re += sens_re * back_re + sens_im * back_im
+            grad_im += sens_re * back_im - sens_im * back_re
     scaled = step * (1.0 / ACCEL)
     return image_re - scaled * grad_re, image_im - scaled * grad_im
 
@@ -425,6 +430,7 @@
         z_high, z_low, maybe = {
             "a": (near, far, False), "b": (near, near, False), "c": (far, near, True), "d": (far, far, True),
             "3": (near, 1 - step_in, False), "2": (near, step_in, False), "1": (far, 1 - step_in, False), "0": (far, step_in, True),
+            "W": (0, 0, True), "X": (0, 1, True), "Y": (1, 0, True), "Z": (1, 1, True),
         }[zone]
         for k in reversed(range(quarter)):
             x = lax.rem(inner + k, quarter)
@@ -523,7 +529,7 @@
             inverse[f, f, 1] = jnp.zeros_like(re)
 
     spot = pl.ds(pl.multiple_of(me * rows, rows), rows)
-    for f in range(frames):
+    for f in [0,6,1,7,2,4,3,5]:
         weights = [(inverse[f, g, 0], inverse[f, g, 1]) for g in range(frames)]
         for q in range(group):
             for p in range(planes):

time: 21.7 us -> 21.4 us (0.986)
  Pallas kernels: 19.5 us -> 19.1 us
    pallas_call x1, Pallas kernels: 19.5 us -> 19.1 us  [local_fused(): pl.pallas_call(functools.partial(step_kernel, planes, frames, group, coil...]
where the time goes in v4:
time: 21.4 us; the launch traced here: 21.1 us
  Pallas kernels  19.1 us (89%)
  between operations  1.3 us (6%)
  local copies, waits for them, and re-layouts  0.71 us (3%)
    pallas_call x1, Pallas kernels, local_fused(): pl.pallas_call(functools.partial(step_kernel, planes, frames, group, coil...  19.1 us
    unnamed x1, local copies, waits for them, and re-layouts  0.71 us

profile of v4, /device:TPU:0, one launch (start us, length us, event | category | flops | bytes accessed | tf_op | source)
XLA Modules:
  0.0 21.1 jit_solution(9085082066140678994)
XLA Ops:
  1.3 19.1 %prox_step.1 = f32[2,1,2,128,128]{4,3,2,1,0:T(8,128)S(1)} custom-call(f32[1]{0:T(128)S(6)} %copy.10.step_ref, f32[1]{0:T(128)S(6)} %copy.11.level_ref, s32[2]{0:T(128)} %shifts_hbm.1, s32[1,128]{1,0:T(1,128)} %offsets_hbm.1, f32[2,1,2,128,128]{4,3,2,1,0:T(8,128)} %image_hbm.1, bf16[4,2,2,128,128]{4,3,2,1,0:T(8,128)(2,1)} %sens_hbm.1, ...), custom_call_target="tpu_custom_call" | custom-call | tf_op jit(solution)/shard_map/prox_step/pallas_call | solution.py:586
  20.4 0.7 %copy.12 = f32[2,1,2,128,128]{4,3,2,1,0:T(8,128)} copy(f32[2,1,2,128,128]{4,3,2,1,0:T(8,128)S(1)} %prox_step.1) | data formatting | bytes 524288

commit v5 on v4

--- a/solution.py
+++ b/solution.py
@@ -529,7 +529,7 @@
             inverse[f, f, 1] = jnp.zeros_like(re)
 
     spot = pl.ds(pl.multiple_of(me * rows, rows), rows)
-    for f in [0,6,1,7,2,4,3,5]:
+    for f in [0, 6, 1, 4, 2, 3, 7, 5]:
         weights = [(inverse[f, g, 0], inverse[f, g, 1]) for g in range(frames)]
         for q in range(group):
             for p in range(planes):

time: 21.4 us -> 21.3 us (level)
  no operation moved by 1% of the time
where the time goes in v5:
time: 21.3 us; the launch traced here: 21.1 us
  Pallas kernels  19.1 us (90%)
  between operations  1.3 us (6%)
  local copies, waits for them, and re-layouts  0.71 us (3%)
    pallas_call x1, Pallas kernels, local_fused(): pl.pallas_call(functools.partial(step_kernel, planes, frames, group, coil...  19.1 us
    unnamed x1, local copies, waits for them, and re-layouts  0.71 us

profile of v5, /device:TPU:0, one launch (start us, length us, event | category | flops | bytes accessed | tf_op | source)
XLA Modules:
  0.0 21.1 jit_solution(12080772070741723907)
XLA Ops:
  1.3 19.1 %prox_step.1 = f32[2,1,2,128,128]{4,3,2,1,0:T(8,128)S(1)} custom-call(f32[1]{0:T(128)S(6)} %copy.10.step_ref, f32[1]{0:T(128)S(6)} %copy.11.level_ref, s32[2]{0:T(128)} %shifts_hbm.1, s32[1,128]{1,0:T(1,128)} %offsets_hbm.1, f32[2,1,2,128,128]{4,3,2,1,0:T(8,128)} %image_hbm.1, bf16[4,2,2,128,128]{4,3,2,1,0:T(8,128)(2,1)} %sens_hbm.1, ...), custom_call_target="tpu_custom_call" | custom-call | tf_op jit(solution)/shard_map/prox_step/pallas_call | solution.py:586
  20.4 0.7 %copy.12 = f32[2,1,2,128,128]{4,3,2,1,0:T(8,128)} copy(f32[2,1,2,128,128]{4,3,2,1,0:T(8,128)S(1)} %prox_step.1) | data formatting | bytes 524288

commit v6 on v5

--- a/solution.py
+++ b/solution.py
@@ -169,7 +169,7 @@
 VMEM_BYTES = 24 * 1024 * 1024
 
 
-PLAN = [[(0, 'W'), (0, 'Y'), (0, 'X'), (0, 'Z')], [(1, 'W'), (1, 'Y'), (1, 'X'), (1, 'Z')]]
+ZONES = "WYXZ"
 
 
 def two_parts(table):
@@ -222,7 +222,7 @@
     return first[:count] + (first[count:] + mul(table[:count], value_low))
 
 
-def row_patterns(offsets_ref, offset_rows, width_y, width_z):
+def row_patterns(offsets_ref, width_y, width_z):
     lane = lax.broadcasted_iota(jnp.int32, (width_y, width_z), 1)
     row = lax.broadcasted_iota(jnp.int32, (width_y, width_z), 0)
     offset = jnp.broadcast_to(offsets_ref[...].astype(jnp.float32), (width_z, width_y)).T
@@ -415,31 +415,23 @@
             load_plane(p)
 
     loads["offsets"].wait()
-    patterns = row_patterns(offsets_ref, None, width_y, width_z)
+    patterns = row_patterns(offsets_ref, width_y, width_z)
     loads["table"].wait()
     lay_tables(parts_ref, table_ref, width_y)
 
     half, quarter = frames // 2, frames // 4
-    far = frame_me // half
-    near = 1 - far
-    step_in = lax.rem(frame_me // quarter, 2)
     inner = lax.rem(frame_me, quarter)
 
+    first, second, third, last = [list(range(b * quarter, (b + 1) * quarter)) for b in range(4)]
+    order_home = first[:1] + last[:1] + first[1:] + third[:1] + second + last[1:] + third[1:]
+
     def order_out(token):
-        zone, only = token[0], token[1:]
-        z_high, z_low, maybe = {
-            "a": (near, far, False), "b": (near, near, False), "c": (far, near, True), "d": (far, far, True),
-            "3": (near, 1 - step_in, False), "2": (near, step_in, False), "1": (far, 1 - step_in, False), "0": (far, step_in, True),
-            "W": (0, 0, True), "X": (0, 1, True), "Y": (1, 0, True), "Z": (1, 1, True),
-        }[zone]
+        z_high, z_low = {"W": (0, 0), "X": (0, 1), "Y": (1, 0), "Z": (1, 1)}[token]
         for k in reversed(range(quarter)):
             x = lax.rem(inner + k, quarter)
-            if only in ("0", "1"):
-                yield z_high * half + z_low * quarter + x, int(only), maybe and k == 0
-                continue
             for r in reversed(range(group)):
                 q = lax.rem(part_me + r, group)
-                yield z_high * half + z_low * quarter + x, q, maybe and k == 0 and r == 0
+                yield z_high * half + z_low * quarter + x, q, k == 0 and r == 0
 
     def send(p, f, q, maybe):
         block = rolled.at[p, :, pl.ds(pl.multiple_of((f * group + q) * rows, rows), rows), :]
@@ -475,9 +467,9 @@
             gathered.at[p, part_me, frame_me],
             recv_out.at[p],
         ).start()
-        for wp, zone in PLAN[p]:
+        for zone in ZONES:
             for f, q, maybe in order_out(zone):
-                send(wp, f, q, maybe)
+                send(p, f, q, maybe)
 
     pairs = [(f, g) for f in range(frames) for g in range(f + 1)]
     for p in range(planes):
@@ -529,7 +521,7 @@
             inverse[f, f, 1] = jnp.zeros_like(re)
 
     spot = pl.ds(pl.multiple_of(me * rows, rows), rows)
-    for f in [0, 6, 1, 4, 2, 3, 7, 5]:
+    for f in order_home:
         weights = [(inverse[f, g, 0], inverse[f, g, 1]) for g in range(frames)]
         for q in range(group):
             for p in range(planes):
@@ -618,7 +610,7 @@
     planes, frames_dev, _, width_y, width_z = image.shape
     frames = frames_dev * lax.axis_size("frame")
     group = PATCH_X // planes
-    one_block = frames * group * PATCH_Y == width_y and frames_dev == 1 and frames & (frames - 1) == 0
+    one_block = frames * group * PATCH_Y == width_y and frames_dev == 1 and frames & (frames - 1) == 0 and frames >= 4
     split = group > 1 and group & (group - 1) == 0 and lax.axis_size("plane") % group == 0
     if one_block and split and width_y == width_z and width_z % 128 == 0:
         return local_fused(image, sens, kspace, offsets, shifts, step_size, threshold)

time: 21.3 us -> 21.3 us (level)
  no operation moved by 1% of the time
where the time goes in v6:
time: 21.3 us; the launch traced here: 21.1 us
  Pallas kernels  19.1 us (90%)
  between operations  1.3 us (6%)
  local copies, waits for them, and re-layouts  0.71 us (3%)
    pallas_call x1, Pallas kernels, local_fused(): pl.pallas_call(functools.partial(step_kernel, planes, frames, group, coil...  19.1 us
    unnamed x1, local copies, waits for them, and re-layouts  0.71 us

profile of v6, /device:TPU:0, one launch (start us, length us, event | category | flops | bytes accessed | tf_op | source)
XLA Modules:
  0.0 21.1 jit_solution(12080772070741723907)
XLA Ops:
  1.3 19.1 %prox_step.1 = f32[2,1,2,128,128]{4,3,2,1,0:T(8,128)S(1)} custom-call(f32[1]{0:T(128)S(6)} %copy.10.step_ref, f32[1]{0:T(128)S(6)} %copy.11.level_ref, s32[2]{0:T(128)} %shifts_hbm.1, s32[1,128]{1,0:T(1,128)} %offsets_hbm.1, f32[2,1,2,128,128]{4,3,2,1,0:T(8,128)} %image_hbm.1, bf16[4,2,2,128,128]{4,3,2,1,0:T(8,128)(2,1)} %sens_hbm.1, ...), custom_call_target="tpu_custom_call" | custom-call | tf_op jit(solution)/shard_map/prox_step/pallas_call | solution.py:578
  20.4 0.7 %copy.12 = f32[2,1,2,128,128]{4,3,2,1,0:T(8,128)} copy(f32[2,1,2,128,128]{4,3,2,1,0:T(8,128)S(1)} %prox_step.1) | data formatting | bytes 524288

commit v7 on v6

--- a/solution.py
+++ b/solution.py
@@ -384,6 +384,23 @@
     def other(f, q):
         return (frame_me != f) | (part_me != q)
 
+    loads = {}
+
+    def load(name, source, target):
+        loads[name] = pltpu.make_async_copy(source, target, load_sem.at[len(loads)])
+        loads[name].start()
+
+    load("offsets", offsets_hbm, offsets_ref)
+    load("table", table_hbm, parts_ref)
+
+    def load_plane(p):
+        load(("kspace", p), kspace_hbm.at[:, p], kspace_ref.at[:, p])
+        load(("image", p), image_hbm.at[p], image_ref.at[p])
+        load(("sens", p), sens_hbm.at[:, p], sens_ref.at[:, p])
+
+    load_plane(0)
+    load("shifts", shifts_hbm, shifts_ref)
+
     barrier = pltpu.get_barrier_semaphore()
     for f, q in everyone:
 
@@ -392,23 +409,6 @@
             pl.semaphore_signal(
                 barrier, inc=1, device_id={"plane": base + q, "frame": f}, device_id_type=pl.DeviceIdType.MESH
             )
-
-    loads = {}
-
-    def load(name, source, target):
-        loads[name] = pltpu.make_async_copy(source, target, load_sem.at[len(loads)])
-        loads[name].start()
-
-    load("offsets", offsets_hbm, offsets_ref)
-    load("table", table_hbm, parts_ref)
-
-    def load_plane(p):
-        load(("kspace", p), kspace_hbm.at[:, p], kspace_ref.at[:, p])
-        load(("image", p), image_hbm.at[p], image_ref.at[p])
-        load(("sens", p), sens_hbm.at[:, p], sens_ref.at[:, p])
-
-    load_plane(0)
-    load("shifts", shifts_hbm, shifts_ref)
 
     def start_later():
         for p in range(1, planes):

time: 21.3 us -> 21.3 us (level)
  no operation moved by 1% of the time
where the time goes in v7:
time: 21.3 us; the launch traced here: 21.2 us
  Pallas kernels  19.2 us (90%)
  between operations  1.3 us (6%)
  local copies, waits for them, and re-layouts  0.71 us (3%)
    pallas_call x1, Pallas kernels, local_fused(): pl.pallas_call(functools.partial(step_kernel, planes, frames, group, coil...  19.2 us
    unnamed x1, local copies, waits for them, and re-layouts  0.71 us

profile of v7, /device:TPU:0, one launch (start us, length us, event | category | flops | bytes accessed | tf_op | source)
XLA Modules:
  0.0 21.2 jit_solution(17622861272942417416)
XLA Ops:
  1.3 19.2 %prox_step.1 = f32[2,1,2,128,128]{4,3,2,1,0:T(8,128)S(1)} custom-call(f32[1]{0:T(128)S(6)} %copy.10.step_ref, f32[1]{0:T(128)S(6)} %copy.11.level_ref, s32[2]{0:T(128)} %shifts_hbm.1, s32[1,128]{1,0:T(1,128)} %offsets_hbm.1, f32[2,1,2,128,128]{4,3,2,1,0:T(8,128)} %image_hbm.1, bf16[4,2,2,128,128]{4,3,2,1,0:T(8,128)(2,1)} %sens_hbm.1, ...), custom_call_target="tpu_custom_call" | custom-call | tf_op jit(solution)/shard_map/prox_step/pallas_call | solution.py:578
  20.5 0.7 %copy.12 = f32[2,1,2,128,128]{4,3,2,1,0:T(8,128)} copy(f32[2,1,2,128,128]{4,3,2,1,0:T(8,128)S(1)} %prox_step.1) | data formatting | bytes 524288
